TPU v7x, 256 devices: a whole 4x4x8 slice. The times are simulated.
256 devices in a mesh: dp: 16 (over y, x_hi, core), mp: 16 (over z, x_lo).
Axes of the slice: x: 4 (x_hi: 2, x_lo: 2; x = x_hi * 2 + x_lo), y: 4, z: 8, core: 2. Of those that a mesh axis runs over, the one named last changes fastest.
Arguments:
- tokens: bfloat16 [16384, 2048], P(('dp', 'mp')), may hold values from -6 to 6
- norm_gain: float32 [2048], replicated, may hold values from 0.1 to 1.9
- mlp_gain: float32 [2048], replicated, may hold values from 0.1 to 1.9
- lengths: int32 [16], P('dp'), may hold values from 1 to 1024, as said below
- log_decay: float32 [16384, 8], P('dp'), as said below
- query_master: float32 [2048, 2048], P(('dp', 'mp')), may hold values from -0.125 to 0.125
- key_master: float32 [2048, 2048], P(('dp', 'mp')), may hold values from -0.125 to 0.125
- value_master: float32 [2048, 4096], P(('dp', 'mp')), may hold values from -0.125 to 0.125
- swish_master: float32 [2048, 4096], P(('dp', 'mp')), may hold values from -0.125 to 0.125
- output_master: float32 [4096, 2048], P(None, ('dp', 'mp')), may hold values from -0.09375 to 0.09375
- ffn_gate_master: float32 [2048, 4096], P(('dp', 'mp')), may hold values from -0.125 to 0.125
- ffn_up_master: float32 [2048, 4096], P(('dp', 'mp')), may hold values from -0.125 to 0.125
Outputs:
- residual: bfloat16 [16384, 2048], P(('dp', 'mp'))
- hidden: bfloat16 [16384, 4096], P('dp', 'mp')
Inputs may be any that keep to these rules, and one draw needn't show every extreme that they name: `lengths`: given length of each prompt; in every draw some prompt has exactly 1024 tokens and some has 1. `log_decay`: Negative.
All inputs are finite; a program needn't handle non-finite values.
Results may differ from a plain program's by a relative error of at most 0.023.
Values may be sent and summed in bfloat16 or wider, within the bound.
A program may use at most 128 MiB of HBM per device.

v0:
```python
import math
import jax
import jax.numpy as jnp
from jax import lax
from jax.sharding import PartitionSpec as P

H = 8
DK = 256
DV = 512
REQUEST_SPAN = 1024
BLOCK = 512
PROMPTS_DP = 1


def rms_rows(row_block, gain_vec):
    values = row_block.astype(jnp.float32)
    scale = lax.rsqrt(jnp.mean(values * values, axis=-1, keepdims=True) + 1e-06)
    return (values * scale * gain_vec).astype(jnp.bfloat16)


def rotate(values, places):
    columns = values.shape[1]
    channel = jnp.arange(columns, dtype=jnp.int32) % DK
    paired = (channel // 2 * 2).astype(jnp.float32)
    frequency = jnp.exp(paired * (-math.log(10000.0) / DK))
    angles = places.astype(jnp.float32)[:, None] * frequency[None, :]
    couples = values.reshape(values.shape[0], columns // 2, 2)
    turned = jnp.stack([-couples[:, :, 1], couples[:, :, 0]], axis=-1).reshape(values.shape)
    return values * jnp.cos(angles) + turned * jnp.sin(angles)


def spread_heads(matrix, width, copies):
    row_total = matrix.shape[0]
    per_head = jnp.repeat(matrix.reshape(row_total, H, width), copies, axis=1)
    return per_head.reshape(row_total, H * copies * width)


def trainer_order(block_rows, dp_count, mp_count):
    row_total, columns = block_rows.shape
    split_rows = block_rows.reshape(mp_count, dp_count, row_total // (dp_count * mp_count), columns)
    return split_rows.transpose(1, 0, 2, 3).reshape(row_total, columns)


def retain_block(offset, q_block, k_block, v_block, run_query, run_key):
    scores = jnp.einsum(
        "thd,shd->hts", q_block, k_block, preferred_element_type=jnp.float32
    ) * DK ** (-0.5)
    decay_gap = run_query.T[:, :, None] - run_key.T[:, None, :]
    causal_mask = (offset + jnp.arange(q_block.shape[0], dtype=jnp.int32))[:, None] >= jnp.arange(
        k_block.shape[0], dtype=jnp.int32
    )[None, :]
    weights = (scores * jnp.exp(jnp.where(causal_mask[None], decay_gap, -jnp.inf))).astype(
        jnp.bfloat16
    )
    return jnp.einsum("hts,shd->thd", weights, v_block, preferred_element_type=jnp.float32)


def per_device(
    tokens,
    norm_gain,
    mlp_gain,
    lengths,
    log_decay,
    query_master,
    key_master,
    value_master,
    swish_master,
    output_master,
    ffn_gate_master,
    ffn_up_master,
):
    mp_count = lax.axis_size("mp")
    dp_count = lax.axis_size("dp")
    mp_index = lax.axis_index("mp")
    head_share = max(1, mp_count // H)
    local_heads = max(1, H // mp_count)
    partner_bit = mp_index % head_share
    group_rows = PROMPTS_DP * REQUEST_SPAN
    value_width = DV // head_share
    m_query = spread_heads(query_master.astype(jnp.bfloat16), DK, head_share)
    m_key = spread_heads(key_master.astype(jnp.bfloat16), DK, head_share)
    m_value = spread_heads(value_master.astype(jnp.bfloat16), DV, head_share)
    m_swish = swish_master.astype(jnp.bfloat16)
    m_output = output_master.T.astype(jnp.bfloat16)
    m_ffn_gate = ffn_gate_master.astype(jnp.bfloat16)
    m_ffn_up = ffn_up_master.astype(jnp.bfloat16)
    r_query, r_key, r_value, r_swish, r_output, r_gate, r_up = (
        lax.all_gather(m_query, "dp", axis=0, tiled=True),
        lax.all_gather(m_key, "dp", axis=0, tiled=True),
        lax.all_gather(m_value, "dp", axis=0, tiled=True),
        lax.all_gather(m_swish, "dp", axis=0, tiled=True),
        lax.all_gather(m_output, "dp", axis=0, tiled=True),
        lax.all_gather(m_ffn_gate, "dp", axis=0, tiled=True),
        lax.all_gather(m_ffn_up, "dp", axis=0, tiled=True),
    )
    owned_parts = (
        lax.all_to_all(r_query, "mp", split_axis=1, concat_axis=0, tiled=True),
        lax.all_to_all(r_key, "mp", split_axis=1, concat_axis=0, tiled=True),
        lax.all_to_all(r_value, "mp", split_axis=1, concat_axis=0, tiled=True),
        lax.all_to_all(r_swish, "mp", split_axis=1, concat_axis=0, tiled=True),
        lax.all_to_all(r_output, "mp", split_axis=1, concat_axis=0, tiled=True),
        lax.all_to_all(r_gate, "mp", split_axis=1, concat_axis=0, tiled=True),
        lax.all_to_all(r_up, "mp", split_axis=1, concat_axis=0, tiled=True),
    )
    server = [trainer_order(owned, dp_count, mp_count) for owned in owned_parts]
    w_query, w_key, w_value, w_swish, w_output, w_ffn_gate, w_ffn_up = server
    width_qk = w_query.shape[1]
    width_value = w_value.shape[1]
    merged_weights = jnp.concatenate([w_query, w_key, w_value, w_swish], axis=1)
    normed_in = rms_rows(tokens, norm_gain)
    shard_piece = lax.all_gather(normed_in, "mp", axis=0, tiled=True)
    places = jnp.arange(shard_piece.shape[0], dtype=jnp.int32) % REQUEST_SPAN
    projected_rows = jnp.dot(shard_piece, merged_weights, preferred_element_type=jnp.float32)
    rotated_query = rotate(projected_rows[:, :width_qk], places)
    rotated_key = rotate(projected_rows[:, width_qk : 2 * width_qk], places)
    projected = jnp.concatenate(
        [rotated_query, rotated_key, projected_rows[:, 2 * width_qk :]], axis=1
    ).astype(jnp.bfloat16)
    queries = projected[:, :width_qk]
    key_rows = projected[:, width_qk : 2 * width_qk]
    value_rows = projected[:, 2 * width_qk : 2 * width_qk + width_value]
    gate_rows = projected[:, 2 * width_qk + width_value :]
    head_first = mp_index // head_share * local_heads
    decay_cols = lax.dynamic_slice_in_dim(log_decay, head_first, local_heads, 1)
    running = jnp.cumsum(decay_cols.reshape(PROMPTS_DP, REQUEST_SPAN, local_heads), axis=1)
    query_four = queries.reshape(PROMPTS_DP, REQUEST_SPAN, local_heads, DK)
    key_four = key_rows.reshape(PROMPTS_DP, REQUEST_SPAN, local_heads, DK)
    value_four = value_rows.reshape(PROMPTS_DP, REQUEST_SPAN, local_heads, DV)

    def one_prompt(prompt_items):
        q_prompt, k_prompt, v_prompt, run_prompt, length_prompt = prompt_items
        outputs = []
        for block_index in range(REQUEST_SPAN // BLOCK):
            low_row = block_index * BLOCK
            top_row = low_row + BLOCK
            operands = (
                q_prompt[low_row:top_row],
                k_prompt[:top_row],
                v_prompt[:top_row],
                run_prompt[low_row:top_row],
                run_prompt[:top_row],
            )
            block_out = retain_block(low_row, *operands)
            outputs.append(block_out)
        return jnp.concatenate(outputs, axis=0)

    retained = lax.map(one_prompt, (query_four, key_four, value_four, running, lengths))
    retained = retained.reshape(group_rows, local_heads, DV)
    channel_mean = jnp.mean(retained, axis=-1, keepdims=True)
    spread = jnp.mean(retained * retained, axis=-1, keepdims=True) - channel_mean * channel_mean
    normed_heads = (retained - channel_mean) * lax.rsqrt(spread + 1e-05)
    normed_heads = lax.dynamic_slice_in_dim(normed_heads, partner_bit * value_width, value_width, 2)
    live_rows = jnp.arange(group_rows, dtype=jnp.int32) % REQUEST_SPAN < jnp.repeat(
        lengths, REQUEST_SPAN
    )
    gated = jnp.where(
        live_rows[:, None],
        jax.nn.silu(gate_rows.astype(jnp.float32))
        * normed_heads.reshape(group_rows, local_heads * value_width),
        0.0,
    ).astype(jnp.bfloat16)
    branch = lax.psum_scatter(
        lax.dot_general(
            gated, w_output, (((1,), (1,)), ((), ())), preferred_element_type=jnp.float32
        ).astype(jnp.bfloat16),
        "mp",
        scatter_dimension=0,
        tiled=True,
    ).astype(jnp.float32)
    residual = (tokens.astype(jnp.float32) + branch).astype(jnp.bfloat16)
    normed_mid = rms_rows(residual, mlp_gain)
    w_gate_up = jnp.concatenate([w_ffn_gate, w_ffn_up], axis=1)
    split_at = w_ffn_gate.shape[1]
    gate_up = jnp.dot(
        lax.all_gather(normed_mid, "mp", axis=0, tiled=True),
        w_gate_up,
        preferred_element_type=jnp.float32,
    )
    hidden = (jax.nn.silu(gate_up[:, :split_at]) * gate_up[:, split_at:]).astype(jnp.bfloat16)
    return (residual, hidden)


def solution(mesh):
    placed = (
        P(("dp", "mp"), None),
        P(),
        P(),
        P("dp"),
        P("dp", None),
        P(("dp", "mp"), None),
        P(("dp", "mp"), None),
        P(("dp", "mp"), None),
        P(("dp", "mp"), None),
        P(None, ("dp", "mp")),
        P(("dp", "mp"), None),
        P(("dp", "mp"), None),
    )
    return jax.shard_map(
        per_device,
        mesh=mesh,
        in_specs=placed,
        out_specs=(P(("dp", "mp"), None), P("dp", "mp")),
        check_vma=False,
    )
```

profile of v0, /device:TPU:1, one launch (start us, length us, event | category | flops | bytes accessed | tf_op | source)
XLA Modules:
  0.0 776.2 jit_solution(15187290181166123529)
XLA Ops:
  10.4 1.5 convert_element_type.99
  12.0 1.5 convert_bitcast_fusion
  13.5 52.0 %all-gather.14.cloned.1.call-done = bf16[128,4096]{1,0:T(8,128)(2,1)} async-done(((bf16[8,4096]{1,0:T(8,128)(2,1)}), bf16[128,4096]{1,0:T(8,128)(2,1)}) %all-gather.14.cloned.1.call-update) | async-done | bytes 1048592 | tf_op jit(solution)/shard_map/all_gather | solution.py:89
  65.5 2.3 copy.66
  67.8 6.8 all-to-all-start.1
  75.4 41.6 %all-gather.12.cloned.1.call-done = bf16[128,4096]{1,0:T(8,128)(2,1)} async-done(((bf16[8,4096]{1,0:T(8,128)(2,1)}), bf16[128,4096]{1,0:T(8,128)(2,1)}) %all-gather.12.cloned.1.call-update) | async-done | bytes 1048592 | tf_op jit(solution)/shard_map/all_gather | solution.py:88
  117.0 2.3 copy.63
  119.3 6.8 all-to-all-start
  126.3 42.8 %all-gather.18.cloned.1.call-done = bf16[128,4096]{1,0:T(8,128)(2,1)} async-done(((bf16[8,4096]{1,0:T(8,128)(2,1)}), bf16[128,4096]{1,0:T(8,128)(2,1)}) %all-gather.18.cloned.1.call-update) | async-done | bytes 1048592 | tf_op jit(solution)/shard_map/all_gather | solution.py:91
  169.1 2.3 copy.72
  171.4 6.8 all-to-all-start.3
  179.1 41.3 %all-gather.20.cloned.1.call-done = bf16[128,4096]{1,0:T(8,128)(2,1)} async-done(((bf16[8,4096]{1,0:T(8,128)(2,1)}), bf16[128,4096]{1,0:T(8,128)(2,1)}) %all-gather.20.cloned.1.call-update) | async-done | bytes 1048592 | tf_op jit(solution)/shard_map/all_gather | solution.py:92
  220.4 2.3 copy.79
  222.7 6.9 all-to-all-start.4
  229.6 45.4 %all-gather.16.cloned.1.call-done = bf16[128,8192]{1,0:T(8,128)(2,1)} async-done(((bf16[8,8192]{1,0:T(8,128)(2,1)}), bf16[128,8192]{1,0:T(8,128)(2,1)}) %all-gather.16.cloned.1.call-update) | async-done | bytes 2097168 | tf_op jit(solution)/shard_map/all_gather | solution.py:90
  275.0 4.1 copy.69
  279.1 6.8 all-to-all-start.2
  287.7 1.3 copy.67
  289.0 2.4 copy.68
  291.4 1.3 copy.64
  292.8 2.4 copy.65
  295.1 1.3 copy.73
  296.5 2.4 copy.74
  298.8 1.5 copy.80
  301.4 49.0 %all-to-all-done.2 = bf16[128,16,512]{0,2,1:T(8,128)(2,1)S(1)} async-done(((bf16[128,16,512]{0,2,1:T(8,128)(2,1)}), bf16[128,16,512]{0,2,1:T(8,128)(2,1)S(1)}, u32[]{:S(2)}, u32[]{:S(2)}) %all-to-all-start.2) | async-done | bytes 2097184 | tf_op jit(solution)/shard_map/all_to_all | solution.py:99
  350.4 2.6 copy.70
  353.0 1.9 copy.71
  354.9 52.4 %all-gather.10.cloned.1.call-done = bf16[1024,2048]{1,0:T(8,128)(2,1)} async-done(((bf16[64,2048]{1,0:T(8,128)(2,1)}), bf16[1024,2048]{1,0:T(8,128)(2,1)}) %all-gather.10.cloned.1.call-update) | async-done | bytes 4194320 | tf_op jit(solution)/shard_map/all_gather | solution.py:111
  407.3 9.9 %fusion.85 = (bf16[1024,1280]{1,0:T(8,128)(2,1)}, f32[1024,1280]{1,0:T(8,128)S(1)}) fusion(bf16[1024,2048]{1,0:T(8,128)(2,1)} %all-gather.10.cloned.1.call-done, bf16[2048,256]{1,0:T(8,128)(2,1)} %bitcast.111, bf16[2048,512]{1,0:T(8,128)(2,1)S(1)} %bitcast.107, bf16[2048,256]{1,0:T(8,128)(2,1)S(1)} %bitcast.109, bf16[2048,256]{1,0:T(8,128)(2,1)} %bitcast.110), kind=kOutput, calls=%fused_computation.126 | convolution fusion | flops 5390991360 | bytes 17301504 | tf_op jit(solution)/shard_map/dot_general | solution.py:113
  417.2 1.2 fusion.84
  418.4 1.4 copy-done.6
  423.6 1.6 copy.75
  428.7 7.1 fusion.25
  436.8 1.7 convolution_bitcast_fusion.1
  438.4 2.7 convolution_bitcast_fusion
  441.5 4.5 convolution_convert_fusion
  448.4 96.5 %reduce-scatter.2.cloned.1.call-done = bf16[64,2048]{1,0:T(8,128)(2,1)} async-done(((bf16[1024,2048]{1,0:T(8,128)(2,1)}), bf16[64,2048]{1,0:T(8,128)(2,1)}) %reduce-scatter.2.cloned.1.call-update) | async-done | bytes 262160 | tf_op jit(solution)/shard_map/reduce_scatter | solution.py:162
  544.9 1.1 fusion.43
  546.9 52.9 %all-gather.24.cloned.1.call-done = bf16[128,4096]{1,0:T(8,128)(2,1)} async-done(((bf16[8,4096]{1,0:T(8,128)(2,1)}), bf16[128,4096]{1,0:T(8,128)(2,1)}) %all-gather.24.cloned.1.call-update) | async-done | bytes 1048592 | tf_op jit(solution)/shard_map/all_gather | solution.py:93
  599.8 2.3 copy.82
  602.1 6.8 all-to-all-start.5
  608.9 42.4 %all-gather.26.cloned.1.call-done = bf16[128,4096]{1,0:T(8,128)(2,1)} async-done(((bf16[8,4096]{1,0:T(8,128)(2,1)}), bf16[128,4096]{1,0:T(8,128)(2,1)}) %all-gather.26.cloned.1.call-update) | async-done | bytes 1048592 | tf_op jit(solution)/shard_map/all_gather | solution.py:94
  651.3 2.3 copy.85
  653.6 6.8 all-to-all-start.6
  662.1 31.7 %all-to-all-done.6 = bf16[128,16,256]{0,2,1:T(8,128)(2,1)S(1)} async-done(((bf16[128,16,256]{0,2,1:T(8,128)(2,1)}), bf16[128,16,256]{0,2,1:T(8,128)(2,1)S(1)}, u32[]{:S(2)}, u32[]{:S(2)}) %all-to-all-start.6) | async-done | bytes 1048608 | tf_op jit(solution)/shard_map/all_to_all | solution.py:103
  694.4 69.3 %all-gather.22.cloned.1.call-done = bf16[1024,2048]{1,0:T(8,128)(2,1)} async-done(((bf16[64,2048]{1,0:T(8,128)(2,1)}), bf16[1024,2048]{1,0:T(8,128)(2,1)}) %all-gather.22.cloned.1.call-update) | async-done | bytes 4194320 | tf_op jit(solution)/shard_map/all_gather | solution.py:175
  763.7 4.5 fusion.8
  768.2 1.1 fusion.32
  (107 shorter events, 21.0 us)
Async XLA Ops:
  7.2 278.9 %copy-start = (f32[1024,8]{0,1:T(8,128)S(1)}, f32[1024,8]{0,1:T(8,128)}, u32[]{:S(2)}) copy-start(f32[1024,8]{0,1:T(8,128)} %param.16) | copy-start | bytes 98308
  7.2 67.5 %copy-start.14 = (f32[8,4096]{1,0:T(8,128)S(1)}, f32[8,4096]{1,0:T(8,128)}, u32[]{:S(2)}) copy-start(f32[8,4096]{1,0:T(8,128)} %param.19) | copy-start | bytes 393220
  7.2 58.3 %all-gather.14.cloned.1.call-start = ((), (), s32[]{:S(2)}) async-start(), calls=%async_computation.10 | async-start | bytes 1114112 | tf_op jit(solution)/shard_map/all_gather | solution.py:89
  8.8 108.2 %all-gather.12.cloned.1.call-start = ((), (), s32[]{:S(2)}) async-start(), calls=%async_computation.9 | async-start | bytes 1114112 | tf_op jit(solution)/shard_map/all_gather | solution.py:88
  10.3 158.7 %all-gather.18.cloned.1.call-start = ((), (), s32[]{:S(2)}) async-start(), calls=%async_computation.12 | async-start | bytes 1114112 | tf_op jit(solution)/shard_map/all_gather | solution.py:91
  11.9 208.5 %all-gather.20.cloned.1.call-start = ((), (), s32[]{:S(2)}) async-start(), calls=%async_computation.13 | async-start | bytes 1114112 | tf_op jit(solution)/shard_map/all_gather | solution.py:92
  67.8 51.5 %all-to-all-start.1 = ((bf16[128,16,256]{0,2,1:T(8,128)(2,1)}), bf16[128,16,256]{0,2,1:T(8,128)(2,1)S(1)}, u32[]{:S(2)}, u32[]{:S(2)}) async-start(bf16[128,16,256]{0,2,1:T(8,128)(2,1)} %bitcast.10), calls=%async_computation.1 | async-start | bytes 2097152 | tf_op jit(solution)/shard_map/all_to_all | solution.py:98
  74.6 51.5 %copy-start.7 = (bf16[64,2048]{1,0:T(8,128)(2,1)S(1)}, bf16[64,2048]{1,0:T(8,128)(2,1)}, u32[]{:S(2)}) copy-start(bf16[64,2048]{1,0:T(8,128)(2,1)} %param.12) | copy-start | bytes 786436
  74.7 200.4 %all-gather.16.cloned.1.call-start = ((), (), s32[]{:S(2)}) async-start(), calls=%async_computation.11 | async-start | bytes 2228224 | tf_op jit(solution)/shard_map/all_gather | solution.py:90
  119.3 52.1 %all-to-all-start = ((bf16[128,16,256]{0,2,1:T(8,128)(2,1)}), bf16[128,16,256]{0,2,1:T(8,128)(2,1)S(1)}, u32[]{:S(2)}, u32[]{:S(2)}) async-start(bf16[128,16,256]{0,2,1:T(8,128)(2,1)} %bitcast.3), calls=%async_computation | async-start | bytes 2097152 | tf_op jit(solution)/shard_map/all_to_all | solution.py:97
  126.1 52.1 %copy-start.17 = (f32[2048]{0:T(1024)S(1)}, f32[2048]{0:T(1024)}, u32[]{:S(2)}) copy-start(f32[2048]{0:T(1024)} %param.13) | copy-start | bytes 24580
  171.4 51.3 %copy-start.2 = (bf16[128,16,256]{0,2,1:T(8,128)(2,1)}, bf16[128,16,256]{0,2,1:T(8,128)(2,1)S(1)}, u32[]{:S(2)}) copy-start(bf16[128,16,256]{0,2,1:T(8,128)(2,1)S(1)} %all-to-all-done) | copy-start | bytes 3145732
  171.4 51.3 %all-to-all-start.3 = ((bf16[128,16,256]{0,2,1:T(8,128)(2,1)}), bf16[128,16,256]{0,2,1:T(8,128)(2,1)S(1)}, u32[]{:S(2)}, u32[]{:S(2)}) async-start(bf16[128,16,256]{0,2,1:T(8,128)(2,1)} %bitcast.97), calls=%async_computation.3 | async-start | bytes 2097152 | tf_op jit(solution)/shard_map/all_to_all | solution.py:100
  178.2 229.1 %all-gather.10.cloned.1.call-start = ((), (), s32[]{:S(2)}) async-start(), calls=%async_computation.8 | async-start | bytes 4456448 | tf_op jit(solution)/shard_map/all_gather | solution.py:111
  222.7 56.5 %copy-start.4 = (bf16[128,16,256]{0,2,1:T(8,128)(2,1)}, bf16[128,16,256]{0,2,1:T(8,128)(2,1)S(1)}, u32[]{:S(2)}) copy-start(bf16[128,16,256]{0,2,1:T(8,128)(2,1)S(1)} %all-to-all-done.3) | copy-start | bytes 3145732
  222.7 56.5 %all-to-all-start.4 = ((bf16[128,16,256]{0,2,1:T(8,128)(2,1)}), bf16[128,16,256]{0,2,1:T(8,128)(2,1)}, u32[]{:S(2)}, u32[]{:S(2)}) async-start(bf16[128,16,256]{0,2,1:T(8,128)(2,1)} %bitcast.99), calls=%async_computation.4 | async-start | bytes 2097152 | tf_op jit(solution)/shard_map/all_to_all | solution.py:101
  279.1 71.3 %all-to-all-start.2 = ((bf16[128,16,512]{0,2,1:T(8,128)(2,1)}), bf16[128,16,512]{0,2,1:T(8,128)(2,1)S(1)}, u32[]{:S(2)}, u32[]{:S(2)}) async-start(bf16[128,16,512]{0,2,1:T(8,128)(2,1)} %bitcast.17), calls=%async_computation.2 | async-start | bytes 4194304 | tf_op jit(solution)/shard_map/all_to_all | solution.py:99
  286.0 258.9 %reduce-scatter.2.cloned.1.call-start = ((), (), s32[]{:S(2)}) async-start(), calls=%async_computation.14 | async-start | bytes 4456448 | tf_op jit(solution)/shard_map/reduce_scatter | solution.py:162
  289.0 2.4 copy-start.3
  292.7 2.4 copy-start.5
  353.0 54.3 %copy-start.9 = (bf16[16,16,8,256]{3,2,1,0:T(8,128)(2,1)S(1)}, bf16[16,16,8,256]{3,2,1,0:T(8,128)(2,1)}, u32[]{:S(2)}) copy-start(bf16[16,16,8,256]{3,2,1,0:T(8,128)(2,1)} %copy.68) | copy-start | bytes 3145732
  417.2 2.6 copy-start.6
  435.8 0.8 copy-start.12
  435.8 1.0 copy-start.13
  438.4 3.1 copy-start.8
  446.0 0.9 copy-start.15
  446.0 1.6 copy-start.16
  446.0 100.0 %copy-start.18 = (f32[2048]{0:T(1024)S(1)}, f32[2048]{0:T(1024)}, u32[]{:S(2)}) copy-start(f32[2048]{0:T(1024)} %param.14) | copy-start | bytes 24580
  446.1 153.7 %all-gather.24.cloned.1.call-start = ((), (), s32[]{:S(2)}) async-start(), calls=%async_computation.16 | async-start | bytes 1114112 | tf_op jit(solution)/shard_map/all_gather | solution.py:93
  447.6 203.7 %all-gather.26.cloned.1.call-start = ((), (), s32[]{:S(2)}) async-start(), calls=%async_computation.17 | async-start | bytes 1114112 | tf_op jit(solution)/shard_map/all_gather | solution.py:94
  448.3 315.4 %all-gather.22.cloned.1.call-start = ((), (), s32[]{:S(2)}) async-start(), calls=%async_computation.15 | async-start | bytes 4456448 | tf_op jit(solution)/shard_map/all_gather | solution.py:175
  546.0 56.1 %copy-start.11 = (bf16[64,2048]{1,0:T(8,128)(2,1)}, bf16[64,2048]{1,0:T(8,128)(2,1)S(1)}, u32[]{:S(2)}) copy-start(bf16[64,2048]{1,0:T(8,128)(2,1)S(1)} %get-tuple-element.17) | copy-start | bytes 786436
  602.1 51.5 %all-to-all-start.5 = ((bf16[128,16,256]{0,2,1:T(8,128)(2,1)}), bf16[128,16,256]{0,2,1:T(8,128)(2,1)S(1)}, u32[]{:S(2)}, u32[]{:S(2)}) async-start(bf16[128,16,256]{0,2,1:T(8,128)(2,1)} %bitcast.46), calls=%async_computation.6 | async-start | bytes 2097152 | tf_op jit(solution)/shard_map/all_to_all | solution.py:102
  653.6 40.2 %all-to-all-start.6 = ((bf16[128,16,256]{0,2,1:T(8,128)(2,1)}), bf16[128,16,256]{0,2,1:T(8,128)(2,1)S(1)}, u32[]{:S(2)}, u32[]{:S(2)}) async-start(bf16[128,16,256]{0,2,1:T(8,128)(2,1)} %bitcast.51), calls=%async_computation.7 | async-start | bytes 2097152 | tf_op jit(solution)/shard_map/all_to_all | solution.py:103
  662.1 101.7 %copy-start.10 = (bf16[16,16,8,256]{3,2,1,0:T(8,128)(2,1)S(1)}, bf16[16,16,8,256]{3,2,1,0:T(8,128)(2,1)}, u32[]{:S(2)}) copy-start(bf16[16,16,8,256]{3,2,1,0:T(8,128)(2,1)} %copy.84) | copy-start | bytes 3145732
  763.7 5.6 copy-start.1
Sparse Core Ops, SparseCore 0:
  11.4 54.1 all-gather.13
  68.3 48.6 all-gather.11
  120.3 48.6 all-gather.17
  171.7 48.6 all-gather.19
  223.6 51.4 all-gather.15
  277.2 130.0 all-gather.9
  446.2 98.6 reduce-scatter.1
  547.6 52.1 all-gather.23
  602.6 48.6 all-gather.25
  653.5 110.1 all-gather.21
where the time goes:
time: 778 us; the launch traced here: 776 us
  waiting for transfers between devices  617 us (79%)
  local copies, waits for them, and re-layouts  50.1 us (6%)
  starting transfers between devices  48.4 us (6%)
  matrix products  23.2 us (3%)
  other arithmetic  21.8 us (3%)
  between operations  15.3 us (2%)
    reduce_scatter x1, waiting for transfers between devices, per_device(): lax.psum_scatter(lax.dot_general(gated, w_output, (((1,), (1,)), ((), ())...  96.5 us
    all_gather x1, waiting for transfers between devices, per_device(): lax.all_gather(normed_mid, 'mp', axis=0, tiled=True)  69.3 us
    all_gather x1, waiting for transfers between devices, per_device(): lax.all_gather(m_ffn_gate, 'dp', axis=0, tiled=True)  52.9 us
    all_gather x1, waiting for transfers between devices, per_device(): shard_piece = lax.all_gather(normed_in, 'mp', axis=0, tiled=True)  52.4 us
    all_gather x1, waiting for transfers between devices, per_device(): lax.all_gather(m_key, 'dp', axis=0, tiled=True)  52 us
    all_to_all x1, waiting for transfers between devices, per_device(): lax.all_to_all(r_value, 'mp', split_axis=1, concat_axis=0, tiled=True)  49 us
    all_gather x1, waiting for transfers between devices, per_device(): lax.all_gather(m_value, 'dp', axis=0, tiled=True)  45.4 us
    all_gather x1, waiting for transfers between devices, per_device(): lax.all_gather(m_swish, 'dp', axis=0, tiled=True)  42.8 us
  transfers between devices with their start and end apart: 17, of which 12 were waited for; matrix products, arithmetic and copies ran while one was open for 6% of the time, Pallas kernels for 0%

commit v1 on v0

--- a/solution.py
+++ b/solution.py
@@ -3,6 +3,7 @@
 import jax.numpy as jnp
 from jax import lax
 from jax.sharding import PartitionSpec as P
+from jax.lax import all_to_all, psum
 
 H = 8
 DK = 256
@@ -10,6 +11,18 @@
 REQUEST_SPAN = 1024
 BLOCK = 512
 PROMPTS_DP = 1
+
+
+def _match_strips_all(z, device_axis):
+    return jnp.concatenate(
+        all_to_all(
+            jnp.stack([z] * psum(1, axis_name=device_axis), axis=0),
+            concat_axis=0,
+            axis_name=device_axis,
+            split_axis=0,
+        ),
+        axis=0,
+    )
 
 
 def rms_rows(row_block, gain_vec):
@@ -88,7 +101,7 @@
         lax.all_gather(m_query, "dp", axis=0, tiled=True),
         lax.all_gather(m_key, "dp", axis=0, tiled=True),
         lax.all_gather(m_value, "dp", axis=0, tiled=True),
-        lax.all_gather(m_swish, "dp", axis=0, tiled=True),
+        _match_strips_all(m_swish, "dp"),
         lax.all_gather(m_output, "dp", axis=0, tiled=True),
         lax.all_gather(m_ffn_gate, "dp", axis=0, tiled=True),
         lax.all_gather(m_ffn_up, "dp", axis=0, tiled=True),

time: 778 us -> 728 us (0.936)
  waiting for transfers between devices: 617 us -> 543 us
  blocking collectives: 0 us -> 25.9 us
    all_gather x1 -> x0, waiting for transfers between devices: 42.8 us -> none  [per_device(): lax.all_gather(m_swish, 'dp', axis=0, tiled=True)]
    all_gather x1, waiting for transfers between devices: 52 us -> 18.1 us  [per_device(): lax.all_gather(m_key, 'dp', axis=0, tiled=True)]
    all_to_all x0 -> x1, blocking collectives: none -> 25.9 us  [_match_strips_all(): all_to_all(jnp.stack([z] * psum(1, axis_name=device_axis), axis=0), conca...]
  transfers between devices with their start and end apart: 17 -> 16, of which waited for: 12 -> 12; matrix products, arithmetic and copies ran while one was open for 6% -> 6% of each run, Pallas kernels for 0% -> 0%
where the time goes in v1:
time: 728 us; the launch traced here: 726 us
  waiting for transfers between devices  543 us (75%)
  starting transfers between devices  50 us (7%)
  local copies, waits for them, and re-layouts  48.6 us (7%)
  blocking collectives  25.9 us (4%)
  matrix products  23.2 us (3%)
  other arithmetic  21.1 us (3%)
  between operations  15 us (2%)
    reduce_scatter x1, waiting for transfers between devices, per_device(): lax.psum_scatter(lax.dot_general(gated, w_output, (((1,), (1,)), ((), ())...  96.7 us
    all_gather x1, waiting for transfers between devices, per_device(): lax.all_gather(normed_mid, 'mp', axis=0, tiled=True)  69.9 us
    all_gather x1, waiting for transfers between devices, per_device(): shard_piece = lax.all_gather(normed_in, 'mp', axis=0, tiled=True)  54.4 us
    all_gather x1, waiting for transfers between devices, per_device(): lax.all_gather(m_ffn_gate, 'dp', axis=0, tiled=True)  51.9 us
    all_to_all x1, waiting for transfers between devices, per_device(): lax.all_to_all(r_value, 'mp', split_axis=1, concat_axis=0, tiled=True)  48.6 us
    all_gather x1, waiting for transfers between devices, per_device(): lax.all_gather(m_value, 'dp', axis=0, tiled=True)  45.4 us
    all_gather x1, waiting for transfers between devices, per_device(): lax.all_gather(m_ffn_up, 'dp', axis=0, tiled=True)  42.4 us
    all_gather x1, waiting for transfers between devices, per_device(): lax.all_gather(m_output, 'dp', axis=0, tiled=True)  41.4 us
  transfers between devices with their start and end apart: 16, of which 12 were waited for; matrix products, arithmetic and copies ran while one was open for 6% of the time, Pallas kernels for 0%

profile of v1, /device:TPU:1, one launch (start us, length us, event | category | flops | bytes accessed | tf_op | source)
XLA Modules:
  0.0 726.4 jit_solution(722321175579754053)
XLA Ops:
  10.3 1.5 convert_bitcast_fusion
  12.9 25.9 %all_to_all.117 = bf16[16,8,4096]{2,1,0:T(8,128)(2,1)S(1)} all-to-all(bf16[16,8,4096]{2,1,0:T(8,128)(2,1)S(1)} %stack.6), channel_id=1, replica_groups=mesh['dp'=16,'mp'=16] {'dp'}, dimensions={0} | all-to-all | bytes 2097152 | tf_op jit(solution)/shard_map/all_to_all | solution.py:18
  39.0 1.3 copy.73
  40.4 8.3 %all-to-all-start.4 = ((bf16[128,16,256]{2,0,1:T(8,128)(2,1)}), bf16[128,16,256]{2,0,1:T(8,128)(2,1)S(1)}, u32[]{:S(2)}, u32[]{:S(2)}) async-start(bf16[128,16,256]{2,0,1:T(8,128)(2,1)} %copy.73), calls=%async_computation.4 | async-start | bytes 2097152 | tf_op jit(solution)/shard_map/all_to_all | solution.py:113
  49.5 18.1 %all-gather.13.cloned.1.call-done = bf16[128,4096]{1,0:T(8,128)(2,1)} async-done(((bf16[8,4096]{1,0:T(8,128)(2,1)}), bf16[128,4096]{1,0:T(8,128)(2,1)}) %all-gather.13.cloned.1.call-update) | async-done | bytes 1048592 | tf_op jit(solution)/shard_map/all_gather | solution.py:102
  67.6 2.3 copy.67
  69.8 3.4 all-to-all-done.4
  73.3 7.1 all-to-all-start.1
  80.5 38.5 %all-gather.11.cloned.1.call-done = bf16[128,4096]{1,0:T(8,128)(2,1)} async-done(((bf16[8,4096]{1,0:T(8,128)(2,1)}), bf16[128,4096]{1,0:T(8,128)(2,1)}) %all-gather.11.cloned.1.call-update) | async-done | bytes 1048592 | tf_op jit(solution)/shard_map/all_gather | solution.py:101
  119.0 2.3 copy.64
  121.4 6.8 all-to-all-start
  129.1 41.4 %all-gather.17.cloned.1.call-done = bf16[128,4096]{1,0:T(8,128)(2,1)} async-done(((bf16[8,4096]{1,0:T(8,128)(2,1)}), bf16[128,4096]{1,0:T(8,128)(2,1)}) %all-gather.17.cloned.1.call-update) | async-done | bytes 1048592 | tf_op jit(solution)/shard_map/all_gather | solution.py:105
  170.5 2.3 copy.79
  172.8 6.9 all-to-all-start.5
  179.7 45.4 %all-gather.15.cloned.1.call-done = bf16[128,8192]{1,0:T(8,128)(2,1)} async-done(((bf16[8,8192]{1,0:T(8,128)(2,1)}), bf16[128,8192]{1,0:T(8,128)(2,1)}) %all-gather.15.cloned.1.call-update) | async-done | bytes 2097168 | tf_op jit(solution)/shard_map/all_gather | solution.py:103
  225.1 4.1 copy.70
  229.2 6.8 all-to-all-start.2
  237.8 1.1 copy.74
  238.9 2.4 copy.68
  241.3 2.3 copy.69
  243.6 1.3 copy.65
  244.9 2.4 copy.66
  247.2 1.5 copy.80
  249.8 48.6 %all-to-all-done.2 = bf16[128,16,512]{0,2,1:T(8,128)(2,1)S(1)} async-done(((bf16[128,16,512]{0,2,1:T(8,128)(2,1)}), bf16[128,16,512]{0,2,1:T(8,128)(2,1)S(1)}, u32[]{:S(2)}, u32[]{:S(2)}) %all-to-all-start.2) | async-done | bytes 2097184 | tf_op jit(solution)/shard_map/all_to_all | solution.py:112
  298.4 2.6 copy.71
  301.1 1.9 copy.72
  303.0 54.4 %all-gather.9.cloned.1.call-done = bf16[1024,2048]{1,0:T(8,128)(2,1)} async-done(((bf16[64,2048]{1,0:T(8,128)(2,1)}), bf16[1024,2048]{1,0:T(8,128)(2,1)}) %all-gather.9.cloned.1.call-update) | async-done | bytes 4194320 | tf_op jit(solution)/shard_map/all_gather | solution.py:124
  357.3 9.9 %fusion.85 = (bf16[1024,1280]{1,0:T(8,128)(2,1)}, f32[1024,1280]{1,0:T(8,128)S(1)}) fusion(bf16[1024,2048]{1,0:T(8,128)(2,1)} %all-gather.9.cloned.1.call-done, bf16[2048,256]{1,0:T(8,128)(2,1)S(1)} %bitcast.113, bf16[2048,512]{1,0:T(8,128)(2,1)S(1)} %bitcast.111, bf16[2048,256]{1,0:T(8,128)(2,1)} %bitcast.114, bf16[2048,256]{1,0:T(8,128)(2,1)} %bitcast.115), kind=kOutput, calls=%fused_computation.126 | convolution fusion | flops 5390991360 | bytes 17301504 | tf_op jit(solution)/shard_map/dot_general | solution.py:126
  367.2 1.2 fusion.84
  368.4 1.4 copy-done.5
  373.7 1.6 copy.75
  378.7 7.1 fusion.25
  386.8 1.7 convolution_bitcast_fusion.1
  388.5 2.7 convolution_bitcast_fusion
  391.6 4.5 convolution_convert_fusion
  398.4 96.7 %reduce-scatter.2.cloned.1.call-done = bf16[64,2048]{1,0:T(8,128)(2,1)} async-done(((bf16[1024,2048]{1,0:T(8,128)(2,1)}), bf16[64,2048]{1,0:T(8,128)(2,1)}) %reduce-scatter.2.cloned.1.call-update) | async-done | bytes 262160 | tf_op jit(solution)/shard_map/reduce_scatter | solution.py:175
  495.1 1.1 fusion.43
  497.9 51.9 %all-gather.21.cloned.1.call-done = bf16[128,4096]{1,0:T(8,128)(2,1)} async-done(((bf16[8,4096]{1,0:T(8,128)(2,1)}), bf16[128,4096]{1,0:T(8,128)(2,1)}) %all-gather.21.cloned.1.call-update) | async-done | bytes 1048592 | tf_op jit(solution)/shard_map/all_gather | solution.py:106
  549.8 2.3 copy.82
  552.1 6.8 all-to-all-start.6
  558.9 42.4 %all-gather.23.cloned.1.call-done = bf16[128,4096]{1,0:T(8,128)(2,1)} async-done(((bf16[8,4096]{1,0:T(8,128)(2,1)}), bf16[128,4096]{1,0:T(8,128)(2,1)}) %all-gather.23.cloned.1.call-update) | async-done | bytes 1048592 | tf_op jit(solution)/shard_map/all_gather | solution.py:107
  601.3 2.3 copy.85
  603.6 6.8 all-to-all-start.7
  611.0 1.1 copy.84
  612.1 31.6 %all-to-all-done.7 = bf16[128,16,256]{0,2,1:T(8,128)(2,1)S(1)} async-done(((bf16[128,16,256]{0,2,1:T(8,128)(2,1)}), bf16[128,16,256]{0,2,1:T(8,128)(2,1)S(1)}, u32[]{:S(2)}, u32[]{:S(2)}) %all-to-all-start.7) | async-done | bytes 1048608 | tf_op jit(solution)/shard_map/all_to_all | solution.py:116
  644.3 69.9 %all-gather.19.cloned.1.call-done = bf16[1024,2048]{1,0:T(8,128)(2,1)} async-done(((bf16[64,2048]{1,0:T(8,128)(2,1)}), bf16[1024,2048]{1,0:T(8,128)(2,1)}) %all-gather.19.cloned.1.call-update) | async-done | bytes 4194320 | tf_op jit(solution)/shard_map/all_gather | solution.py:188
  714.2 4.5 fusion.8
  718.7 1.1 fusion.32
  (104 shorter events, 21.8 us)
Async XLA Ops:
  7.2 229.0 %copy-start = (f32[1024,8]{0,1:T(8,128)S(1)}, f32[1024,8]{0,1:T(8,128)}, u32[]{:S(2)}) copy-start(f32[1024,8]{0,1:T(8,128)} %param.16) | copy-start | bytes 98308
  7.2 60.4 %all-gather.13.cloned.1.call-start = ((), (), s32[]{:S(2)}) async-start(), calls=%async_computation.11 | async-start | bytes 1114112 | tf_op jit(solution)/shard_map/all_gather | solution.py:102
  8.7 110.3 %all-gather.11.cloned.1.call-start = ((), (), s32[]{:S(2)}) async-start(), calls=%async_computation.10 | async-start | bytes 1114112 | tf_op jit(solution)/shard_map/all_gather | solution.py:101
  10.3 160.2 %all-gather.17.cloned.1.call-start = ((), (), s32[]{:S(2)}) async-start(), calls=%async_computation.13 | async-start | bytes 1114112 | tf_op jit(solution)/shard_map/all_gather | solution.py:105
  39.0 9.7 %copy-start.13 = (f32[8,4096]{1,0:T(8,128)S(1)}, f32[8,4096]{1,0:T(8,128)}, u32[]{:S(2)}) copy-start(f32[8,4096]{1,0:T(8,128)} %param.19) | copy-start | bytes 393220
  40.4 32.9 %all-to-all-start.4 = ((bf16[128,16,256]{2,0,1:T(8,128)(2,1)}), bf16[128,16,256]{2,0,1:T(8,128)(2,1)S(1)}, u32[]{:S(2)}, u32[]{:S(2)}) async-start(bf16[128,16,256]{2,0,1:T(8,128)(2,1)} %copy.73), calls=%async_computation.4 | async-start | bytes 2097152 | tf_op jit(solution)/shard_map/all_to_all | solution.py:113
  48.7 31.7 %copy-start.6 = (bf16[64,2048]{1,0:T(8,128)(2,1)S(1)}, bf16[64,2048]{1,0:T(8,128)(2,1)}, u32[]{:S(2)}) copy-start(bf16[64,2048]{1,0:T(8,128)(2,1)} %param.12) | copy-start | bytes 786436
  48.7 176.4 %all-gather.15.cloned.1.call-start = ((), (), s32[]{:S(2)}) async-start(), calls=%async_computation.12 | async-start | bytes 2228224 | tf_op jit(solution)/shard_map/all_gather | solution.py:103
  73.3 48.1 %all-to-all-start.1 = ((bf16[128,16,256]{0,2,1:T(8,128)(2,1)}), bf16[128,16,256]{0,2,1:T(8,128)(2,1)S(1)}, u32[]{:S(2)}, u32[]{:S(2)}) async-start(bf16[128,16,256]{0,2,1:T(8,128)(2,1)} %bitcast.10), calls=%async_computation.1 | async-start | bytes 2097152 | tf_op jit(solution)/shard_map/all_to_all | solution.py:111
  80.4 47.9 %copy-start.16 = (f32[2048]{0:T(1024)S(1)}, f32[2048]{0:T(1024)}, u32[]{:S(2)}) copy-start(f32[2048]{0:T(1024)} %param.13) | copy-start | bytes 24580
  121.4 51.4 %copy-start.2 = (bf16[128,16,256]{0,2,1:T(8,128)(2,1)}, bf16[128,16,256]{0,2,1:T(8,128)(2,1)S(1)}, u32[]{:S(2)}) copy-start(bf16[128,16,256]{0,2,1:T(8,128)(2,1)S(1)} %all-to-all-done.1) | copy-start | bytes 3145732
  121.4 51.4 %all-to-all-start = ((bf16[128,16,256]{0,2,1:T(8,128)(2,1)}), bf16[128,16,256]{0,2,1:T(8,128)(2,1)S(1)}, u32[]{:S(2)}, u32[]{:S(2)}) async-start(bf16[128,16,256]{0,2,1:T(8,128)(2,1)} %bitcast.100), calls=%async_computation | async-start | bytes 2097152 | tf_op jit(solution)/shard_map/all_to_all | solution.py:110
  128.2 229.1 %all-gather.9.cloned.1.call-start = ((), (), s32[]{:S(2)}) async-start(), calls=%async_computation.9 | async-start | bytes 4456448 | tf_op jit(solution)/shard_map/all_gather | solution.py:124
  172.8 56.5 %copy-start.3 = (bf16[128,16,256]{0,2,1:T(8,128)(2,1)}, bf16[128,16,256]{0,2,1:T(8,128)(2,1)S(1)}, u32[]{:S(2)}) copy-start(bf16[128,16,256]{0,2,1:T(8,128)(2,1)S(1)} %all-to-all-done) | copy-start | bytes 3145732
  172.8 56.5 %all-to-all-start.5 = ((bf16[128,16,256]{0,2,1:T(8,128)(2,1)}), bf16[128,16,256]{0,2,1:T(8,128)(2,1)}, u32[]{:S(2)}, u32[]{:S(2)}) async-start(bf16[128,16,256]{0,2,1:T(8,128)(2,1)} %bitcast.102), calls=%async_computation.5 | async-start | bytes 2097152 | tf_op jit(solution)/shard_map/all_to_all | solution.py:114
  229.2 69.2 %all-to-all-start.2 = ((bf16[128,16,512]{0,2,1:T(8,128)(2,1)}), bf16[128,16,512]{0,2,1:T(8,128)(2,1)S(1)}, u32[]{:S(2)}, u32[]{:S(2)}) async-start(bf16[128,16,512]{0,2,1:T(8,128)(2,1)} %bitcast.17), calls=%async_computation.2 | async-start | bytes 4194304 | tf_op jit(solution)/shard_map/all_to_all | solution.py:112
  236.1 259.1 %reduce-scatter.2.cloned.1.call-start = ((), (), s32[]{:S(2)}) async-start(), calls=%async_computation.14 | async-start | bytes 4456448 | tf_op jit(solution)/shard_map/reduce_scatter | solution.py:175
  238.9 4.7 copy-start.4
  301.1 56.3 %copy-start.8 = (bf16[16,16,8,256]{3,2,1,0:T(8,128)(2,1)S(1)}, bf16[16,16,8,256]{3,2,1,0:T(8,128)(2,1)}, u32[]{:S(2)}) copy-start(bf16[16,16,8,256]{3,2,1,0:T(8,128)(2,1)} %copy.74) | copy-start | bytes 3145732
  367.2 2.7 copy-start.5
  385.8 0.8 copy-start.11
  385.8 1.0 copy-start.12
  388.5 3.1 copy-start.7
  396.1 0.9 copy-start.14
  396.1 1.6 copy-start.15
  396.1 100.9 %copy-start.17 = (f32[2048]{0:T(1024)S(1)}, f32[2048]{0:T(1024)}, u32[]{:S(2)}) copy-start(f32[2048]{0:T(1024)} %param.14) | copy-start | bytes 24580
  396.1 153.7 %all-gather.21.cloned.1.call-start = ((), (), s32[]{:S(2)}) async-start(), calls=%async_computation.16 | async-start | bytes 1114112 | tf_op jit(solution)/shard_map/all_gather | solution.py:106
  397.6 203.7 %all-gather.23.cloned.1.call-start = ((), (), s32[]{:S(2)}) async-start(), calls=%async_computation.17 | async-start | bytes 1114112 | tf_op jit(solution)/shard_map/all_gather | solution.py:107
  398.4 315.8 %all-gather.19.cloned.1.call-start = ((), (), s32[]{:S(2)}) async-start(), calls=%async_computation.15 | async-start | bytes 4456448 | tf_op jit(solution)/shard_map/all_gather | solution.py:188
  496.3 0.7 copy-start.10
  552.1 51.5 %all-to-all-start.6 = ((bf16[128,16,256]{0,2,1:T(8,128)(2,1)}), bf16[128,16,256]{0,2,1:T(8,128)(2,1)S(1)}, u32[]{:S(2)}, u32[]{:S(2)}) async-start(bf16[128,16,256]{0,2,1:T(8,128)(2,1)} %bitcast.45), calls=%async_computation.7 | async-start | bytes 2097152 | tf_op jit(solution)/shard_map/all_to_all | solution.py:115
  603.6 40.1 %all-to-all-start.7 = ((bf16[128,16,256]{0,2,1:T(8,128)(2,1)}), bf16[128,16,256]{0,2,1:T(8,128)(2,1)S(1)}, u32[]{:S(2)}, u32[]{:S(2)}) async-start(bf16[128,16,256]{0,2,1:T(8,128)(2,1)} %bitcast.50), calls=%async_computation.8 | async-start | bytes 2097152 | tf_op jit(solution)/shard_map/all_to_all | solution.py:116
  612.1 102.2 %copy-start.9 = (bf16[16,16,8,256]{3,2,1,0:T(8,128)(2,1)S(1)}, bf16[16,16,8,256]{3,2,1,0:T(8,128)(2,1)}, u32[]{:S(2)}) copy-start(bf16[16,16,8,256]{3,2,1,0:T(8,128)(2,1)} %copy.84) | copy-start | bytes 3145732
  714.2 5.6 copy-start.1
Sparse Core Ops, SparseCore 0:
  11.3 56.1 all-gather.12
  70.3 48.6 all-gather.10
  121.8 48.6 all-gather.16
  173.7 51.4 all-gather.14
  227.3 129.9 all-gather.8
  396.2 98.8 reduce-scatter.1
  497.9 51.8 all-gather.20
  552.6 48.6 all-gather.22
  603.6 110.5 all-gather.18
